TPU v7x, 128 devices: a whole 4x4x4 slice. The times are simulated.
128 devices in a mesh: pop: 8 (over x, core), fsdp: 16 (over y, z).
Axes of the slice: x: 4, y: 4, z: 4, core: 2. Of those that a mesh axis runs over, the one named last changes fastest.
Arguments:
- tokens: bfloat16 [2048, 5120], P('pop', 'fsdp'), may hold values from -6 to 6
- seeds: int32 [2048], replicated, may hold values from 0 to 1048575
- fitness: float32 [2048], P(('pop', 'fsdp')), may hold values from -60 to 60
- gate_weight: bfloat16 [5120, 14336], P('fsdp', 'pop'), may hold values from -0.078125 to 0.078125
- up_weight: bfloat16 [5120, 14336], P('fsdp', 'pop'), may hold values from -0.078125 to 0.078125
- gate_first: float32 [5120, 14336], P('fsdp', 'pop'), may hold values from -4 to 4
- up_first: float32 [5120, 14336], P('fsdp', 'pop'), may hold values from -4 to 4
- gate_second: float32 [5120, 14336], P('fsdp', 'pop'), may hold values from 0.05 to 2
- up_second: float32 [5120, 14336], P('fsdp', 'pop'), may hold values from 0.05 to 2
Outputs:
- hidden: bfloat16 [2048, 14336], P('fsdp', 'pop')
- gate_new: bfloat16 [5120, 14336], P('fsdp', 'pop')
- up_new: bfloat16 [5120, 14336], P('fsdp', 'pop')
- gate_first_new: float32 [5120, 14336], P('fsdp', 'pop')
- up_first_new: float32 [5120, 14336], P('fsdp', 'pop')
- gate_second_new: float32 [5120, 14336], P('fsdp', 'pop')
- up_second_new: float32 [5120, 14336], P('fsdp', 'pop')
All inputs are finite; a program needn't handle non-finite values.
Results may differ from a plain program's by a relative error of at most 0.0022.
Values may be sent and summed in bfloat16 or wider, within the bound.
A program may use at most 128 MiB of HBM per device.

v0:
```python
import functools

import jax
import jax.numpy as jnp
from jax import lax
from jax.experimental import pallas as pl
from jax.experimental.pallas import tpu as pltpu
from jax.sharding import PartitionSpec as P

MESH = pl.DeviceIdType.MESH

noise_scale = 0.01
learn_rate = 0.002
beta_first = 0.9
beta_second = 0.99
adam_floor = 1e-08
stat_epsilon = 1e-06

MEMBERS = 2048
SEED_STEP = 1103515245
COLUMN_STEP = 40503
SALT_STEP = 7919
MIX = 73244475
LEVELS = 32767.0
ROUNDER = 12582912.0


def levels_of(mixed):
    mixed = mixed ^ (mixed >> 15)
    mixed = mixed * MIX
    mixed = mixed ^ (mixed >> 13)
    return (mixed & 255).astype(jnp.float32) - 127.5


def column_of(row, eye):
    return jnp.sum(jnp.where(eye, row, 0.0), axis=1, keepdims=True)


def row_of(column, eye):
    return jnp.sum(jnp.where(eye, column, 0.0), axis=0, keepdims=True)


def remote(src, dst, send_sem, recv_sem, device):
    return pltpu.make_async_remote_copy(
        src_ref=src,
        dst_ref=dst,
        send_sem=send_sem,
        recv_sem=recv_sem,
        device_id=device,
        device_id_type=MESH,
    )


def place(x, c, y, z):
    return {"pop": 2 * lax.rem(x, 4) + c, "fsdp": 4 * lax.rem(y, 4) + lax.rem(z, 4)}


def kernel(
    tokens,
    seeds,
    fitness,
    gate_w,
    up_w,
    hidden,
    grad_gate,
    grad_up,
    xg,
    xk,
    wx,
    info,
    seed_mul,
    scaled,
    ps,
    sc,
    pr,
    sr,
    p0,
    lt,
    wt,
    gb,
    hs,
    ho,
    s_xz,
    r_xz,
    s_xx,
    r_xx,
    l_x,
    s_w,
    r_w,
    s_c,
    r_c,
    s_i,
    r_i,
    s_ic,
    r_ic,
    s_p,
    r_p,
    s_q,
    r_q,
    s_h,
    r_h,
    l_g,
):
    pop = lax.axis_index("pop")
    fsdp = lax.axis_index("fsdp")
    x, c = pop // 2, pop % 2
    y, z = fsdp // 4, fsdp % 4
    width = tokens.shape[1]
    half = wx.shape[3]
    units = 2 * half
    z_core, z_half = z // 2, z % 2
    partner = place(x, 1 - c, y, z)

    barrier = pltpu.get_barrier_semaphore()
    for dc in range(2):
        for dz in range(4):
            if dc or dz:
                pl.semaphore_signal(
                    barrier,
                    inc=1,
                    device_id=place(x, (c + dc) % 2, y, z + dz),
                    device_id_type=MESH,
                )
    for d in range(1, 4):
        pl.semaphore_signal(barrier, inc=1, device_id=place(x + d, c, y, z), device_id_type=MESH)
        pl.semaphore_signal(barrier, inc=1, device_id=place(x, c, y + d, z), device_id_type=MESH)
    pl.semaphore_wait(barrier, 13)

    for d in (1, 3, 2):
        remote(tokens, xg.at[x, z], s_xz.at[d - 1], r_xz.at[d - 1], place(x, c, y, z + d)).start()
    for d in (1, 3, 2):
        remote(
            tokens, xg.at[x, z], s_xx.at[d - 1, 0], r_xx.at[d - 1, 0], place(x + d, c, y, z)
        ).start()
    own = pltpu.make_async_copy(tokens, xg.at[x, z], l_x)
    own.start()

    def weight_send(cm, h):
        src = (gate_w, up_w)[cm].at[:, pl.ds(h * half, half)]
        mine = jnp.logical_and(c == cm, 2 * c + h == z)
        away = remote(
            src, wx.at[cm, z], s_w.at[2 * cm + h], r_w.at[z], place(x, cm, y, 2 * c + h)
        )
        here = pltpu.make_async_copy(src, wx.at[cm, z], r_w.at[z])
        return mine, away, here

    for h in range(2):
        for cm in range(2):
            mine, away, here = weight_send(cm, h)
            pl.when(jnp.logical_not(mine))(away.start)
            pl.when(mine)(here.start)

    eye = lax.broadcasted_iota(jnp.int32, (128, 128), 0) == lax.broadcasted_iota(
        jnp.int32, (128, 128), 1
    )
    seed_mul[...] = seeds[...] * SEED_STEP
    my_info = info.at[c, y, x, z]
    my_info[...] = fitness[...]
    left_columns = (
        lax.broadcasted_iota(jnp.int32, (1, width), 1) + fsdp * width
    ) * COLUMN_STEP
    for b in range(2):
        seed_row = seeds[pl.ds(2 * pop + b, 1), :].astype(jnp.float32)
        seed_col = column_of(seed_row, eye).astype(jnp.int32) * SEED_STEP
        rows = tokens[b * 128 : (b + 1) * 128, :].astype(jnp.float32)
        for k, salt in ((0, 1), (1, 3)):
            left = levels_of(seed_col + (left_columns + salt * SALT_STEP))
            along = jnp.sum(rows * left, axis=1, keepdims=True) * (1.0 / 128.0)
            my_info[1 + 2 * k + b : 2 + 2 * k + b, :] = row_of(along, eye)

    def info_send(stage, ref, d, device):
        return remote(ref, ref, s_i.at[stage, d - 1], r_i.at[stage, d - 1], device)

    for d in range(1, 4):
        info_send(0, info.at[c, y, x, z], d, place(x, c, y, z + d)).start()

    def forward(j):
        piece = xg.at[x, lax.rem(z + 4 - j, 4)]
        remote(piece, piece, s_xz.at[j - 1], r_xz.at[j - 1], place(x, c, y, z + j)).wait_recv()
        for d in (1, 3, 2):
            remote(
                piece, piece, s_xx.at[d - 1, j], r_xx.at[d - 1, j], place(x + d, c, y, z)
            ).start()

    def info_arrived(stage, ref_of):
        for d in range(1, 4):
            info_send(stage, ref_of(d), d, partner).wait_recv()

    for j in (1, 3, 2):
        forward(j)
    info_arrived(0, lambda d: info.at[c, y, x, lax.rem(z + 4 - d, 4)])
    for d in range(1, 4):
        info_send(1, info.at[c, y, x], d, place(x + d, c, y, z)).start()

    sub = lax.broadcasted_iota(jnp.int32, (32, 128), 0)

    def fill_left(k, salt):
        def body(i, _):
            term = (sub + (fsdp * width + i * 32)) * COLUMN_STEP + salt * SALT_STEP
            at = pl.ds(pl.multiple_of(i * 32, 32), 32)
            for r in range(16):
                lt[k, at, r * 128 : (r + 1) * 128] = levels_of(
                    seed_mul[r : r + 1, :] + term
                ).astype(jnp.bfloat16)
            return 0

        lax.fori_loop(0, width // 32, body, 0)

    fill_left(0, 1)
    info_arrived(1, lambda d: info.at[c, y, lax.rem(x + 4 - d, 4)])
    for d in range(1, 4):
        info_send(2, info.at[c, y], d, place(x, c, y + d, z)).start()
    fill_left(1, 3)
    info_arrived(2, lambda d: info.at[c, lax.rem(y + 4 - d, 4)])
    remote(info.at[c], info.at[c], s_ic, r_ic, partner).start()
    remote(info.at[1 - c], info.at[1 - c], s_ic, r_ic, partner).wait_recv()

    lane = lax.broadcasted_iota(jnp.int32, (1, 128), 1) // 16
    for r in range(16):
        p, k = r // 2, r % 2
        row = jnp.zeros((1, 128), jnp.float32)
        for s in range(8):
            tile = info[p % 2, 2 * k + s // 4, p // 2, s % 4, 0:1, :]
            row = jnp.where(lane == s, tile, row)
        scaled[r : r + 1, :] = row
    whole = scaled[...]
    center = jnp.sum(jnp.sum(whole, axis=1, keepdims=True), axis=0, keepdims=True) / MEMBERS
    apart = whole - center
    spread = (
        jnp.sum(jnp.sum(apart * apart, axis=1, keepdims=True), axis=0, keepdims=True) / MEMBERS
    )
    scaled[...] = apart / jnp.sqrt(spread + stat_epsilon)

    chunk = wt.shape[0]

    def gradient(k, salt, first, last):
        def body(i, _):
            def fill(q, _):
                term = (sub + (pop * units + i * chunk + q * 32)) * COLUMN_STEP + salt * SALT_STEP
                at = pl.ds(pl.multiple_of(q * 32, 32), 32)
                for r in range(16):
                    wt[at, r * 128 : (r + 1) * 128] = (
                        levels_of(seed_mul[r : r + 1, :] + term) * scaled[r : r + 1, :]
                    ).astype(jnp.bfloat16)
                return 0

            lax.fori_loop(0, chunk // 32, fill, 0)
            total = lax.dot_general(
                lt[k], wt[...], (((1,), (1,)), ((), ())), preferred_element_type=jnp.float32
            )
            gb[k, :, pl.ds(pl.multiple_of(i * chunk, chunk), chunk)] = total * (
                1.0 / (MEMBERS * noise_scale) / 16384.0
            )
            return 0

        lax.fori_loop(first, last, body, 0)

    chunks = units // chunk
    gradient(0, 2, 0, chunks)
    copy_gate = pltpu.make_async_copy(gb.at[0], grad_gate, l_g.at[0])
    copy_gate.start()
    gradient(1, 4, 0, 2)

    for s in range(4):
        remote(wx.at[c, s], wx.at[c, s], s_w.at[0], r_w.at[s], partner).wait_recv()
        remote(wx.at[c, s], wx.at[c, s], s_c.at[s], r_c.at[s], partner).start()
    own.wait()
    for j in range(4):
        for d in range(1, 4):
            piece = xg.at[lax.rem(x + 4 - d, 4), lax.rem(z + 4 - j, 4)]
            remote(
                piece, piece, s_xx.at[d - 1, j], r_xx.at[d - 1, j], place(x + d, c, y, z)
            ).wait_recv()
    for s in range(4):
        xk[s] = jnp.concatenate([xg[s, j] for j in range(4)], axis=1)
    for s in range(4):
        remote(wx.at[1 - c, s], wx.at[1 - c, s], s_c.at[s], r_c.at[s], partner).wait_recv()

    for d in (2, 1, 3, 0):
        to = lax.rem(y + d, 4)
        rows = xk[to]
        for k in range(2):
            p0[:, k * half : (k + 1) * half] = jnp.dot(
                rows, wx[k].reshape(4 * width, half), preferred_element_type=jnp.float32
            )
        if d == 0:
            break
        for b in range(2):
            at = slice(b * 128, (b + 1) * 128)
            for k in range(2):
                over = slice(k * half, (k + 1) * half)
                top = jnp.max(jnp.abs(p0[at, over]), axis=1, keepdims=True)
                top = jnp.maximum(top, 1e-30)
                grown = p0[at, over] * (LEVELS / top)
                whole_number = (grown + ROUNDER) - ROUNDER
                ps[d - 1, at, over] = whole_number.astype(jnp.int32).astype(jnp.int16)
                sc[d - 1, 2 * k + b : 2 * k + b + 1, :] = row_of(top * (1.0 / LEVELS), eye)
        there = place(x, c, y + d, z)
        remote(ps.at[d - 1], pr.at[d - 1], s_p.at[d - 1], r_p.at[d - 1], there).start()
        remote(sc.at[d - 1], sr.at[d - 1], s_q.at[d - 1], r_q.at[d - 1], there).start()

    gradient(1, 4, 2, chunks)
    copy_up = pltpu.make_async_copy(gb.at[1], grad_up, l_g.at[1])
    copy_up.start()

    for d in (1, 3, 2):
        remote(ps.at[d - 1], pr.at[d - 1], s_p.at[d - 1], r_p.at[d - 1], partner).wait_recv()
        remote(sc.at[d - 1], sr.at[d - 1], s_q.at[d - 1], r_q.at[d - 1], partner).wait_recv()

    first_unit = (2 * x + z_core) * units + z_half * half
    for b in range(2):
        at = slice(b * 128, (b + 1) * 128)
        seed_row = seeds[pl.ds(2 * (2 * y + c) + b, 1), :].astype(jnp.float32)
        seed_col = column_of(seed_row, eye).astype(jnp.int32) * SEED_STEP
        along = []
        for k in range(2):
            row = jnp.zeros((1, 128), jnp.float32)
            for yy in range(4):
                for zz in range(4):
                    row = row + info[c, yy, y, zz, 1 + 2 * k + b : 2 + 2 * k + b, :]
            along.append(column_of(row, eye) * noise_scale)
        steps = [
            [column_of(sr[d, 2 * k + b : 2 * k + b + 1, :], eye) for d in range(3)]
            for k in range(2)
        ]

        def finish(j, _):
            out = []
            for k, salt in ((0, 2), (1, 4)):
                over = pl.ds(pl.multiple_of(k * half + j * 128, 128), 128)
                total = p0[at, over]
                for d in range(3):
                    total = total + pr[d, at, over].astype(jnp.int32).astype(
                        jnp.float32
                    ) * steps[k][d]
                columns = (
                    lax.broadcasted_iota(jnp.int32, (1, 128), 1) + (first_unit + j * 128)
                ) * COLUMN_STEP + salt * SALT_STEP
                right = levels_of(seed_col + columns) * (1.0 / 128.0)
                out.append(total + along[k] * right)
            gate, up = out
            value = gate / (1.0 + jnp.exp(-gate)) * up
            hs[b, :, pl.ds(pl.multiple_of(j * 128, 128), 128)] = value.astype(jnp.bfloat16)
            return 0

        lax.fori_loop(0, half // 128, finish, 0)
        mine = jnp.logical_and(z_core == c, 2 * c + b == z)
        away = remote(
            hs.at[b], ho.at[z_half], s_h.at[b], r_h.at[z_half], place(x, z_core, y, 2 * c + b)
        )
        here = pltpu.make_async_copy(hs.at[b], ho.at[z_half], r_h.at[z_half])
        pl.when(jnp.logical_not(mine))(away.start)
        pl.when(mine)(here.start)

    for h in range(2):
        remote(ho.at[h], ho.at[h], s_h.at[0], r_h.at[h], partner).wait_recv()
        hidden[:, h * half : (h + 1) * half] = ho[h]

    for d in range(1, 4):
        remote(tokens, xg.at[x, z], s_xz.at[d - 1], r_xz.at[d - 1], partner).wait_send()
        for j in range(4):
            remote(tokens, xg.at[x, z], s_xx.at[d - 1, j], r_xx.at[d - 1, j], partner).wait_send()
        info_send(0, info.at[c, y, x, z], d, partner).wait_send()
        info_send(1, info.at[c, y, x], d, partner).wait_send()
        info_send(2, info.at[c, y], d, partner).wait_send()
        remote(ps.at[d - 1], pr.at[d - 1], s_p.at[d - 1], r_p.at[d - 1], partner).wait_send()
        remote(sc.at[d - 1], sr.at[d - 1], s_q.at[d - 1], r_q.at[d - 1], partner).wait_send()
    remote(info.at[c], info.at[c], s_ic, r_ic, partner).wait_send()
    for h in range(2):
        for cm in range(2):
            mine, away, here = weight_send(cm, h)
            pl.when(jnp.logical_not(mine))(away.wait_send)
    for s in range(4):
        remote(wx.at[c, s], wx.at[c, s], s_c.at[s], r_c.at[s], partner).wait_send()
    for b in range(2):
        mine = jnp.logical_and(z_core == c, 2 * c + b == z)
        away = remote(
            hs.at[b], ho.at[z_half], s_h.at[b], r_h.at[z_half], place(x, z_core, y, 2 * c + b)
        )
        pl.when(jnp.logical_not(mine))(away.wait_send)
    copy_gate.wait()
    copy_up.wait()


def adam_step(weight, first, second, grad):
    first_new = beta_first * first + (1.0 - beta_first) * grad
    second_new = beta_second * second + (1.0 - beta_second) * grad * grad
    moved = weight.astype(jnp.float32) + learn_rate * first_new / (
        jnp.sqrt(second_new) + adam_floor
    )
    return (moved.astype(jnp.bfloat16), first_new, second_new)


def shards(
    tokens, seeds, fitness, gate_weight, up_weight, gate_first, up_first, gate_second, up_second
):
    width, units = gate_weight.shape
    half = units // 2
    rows = tokens.shape[0]
    bf, f32, i32, i16 = jnp.bfloat16, jnp.float32, jnp.int32, jnp.int16
    vmem = pl.BlockSpec(memory_space=pltpu.VMEM)
    anywhere = pl.BlockSpec(memory_space=pl.ANY)
    dma = pltpu.SemaphoreType.DMA
    tile = jnp.broadcast_to(jnp.tile(fitness, 8)[None], (8, 128))
    hidden, grad_gate, grad_up = pl.pallas_call(
        kernel,
        name="generation",
        out_shape=(
            jax.ShapeDtypeStruct((rows // 2, units), bf),
            jax.ShapeDtypeStruct((width, units), f32),
            jax.ShapeDtypeStruct((width, units), f32),
        ),
        in_specs=[vmem, vmem, vmem, anywhere, anywhere],
        out_specs=(vmem, anywhere, anywhere),
        scratch_shapes=[
            pltpu.VMEM((4, 4, rows, width), bf),
            pltpu.VMEM((4, rows, 4 * width), bf),
            pltpu.VMEM((2, 4, width, half), bf),
            pltpu.VMEM((2, 4, 4, 4, 8, 128), f32),
            pltpu.VMEM((16, 128), i32),
            pltpu.VMEM((16, 128), f32),
            pltpu.VMEM((3, rows, units), i16),
            pltpu.VMEM((3, 8, 128), f32),
            pltpu.VMEM((3, rows, units), i16),
            pltpu.VMEM((3, 8, 128), f32),
            pltpu.VMEM((rows, units), f32),
            pltpu.VMEM((2, width, MEMBERS), bf),
            pltpu.VMEM((256, MEMBERS), bf),
            pltpu.VMEM((2, width, units), f32),
            pltpu.VMEM((2, rows // 2, half), bf),
            pltpu.VMEM((2, rows // 2, half), bf),
            dma((3,)),
            dma((3,)),
            dma((3, 4)),
            dma((3, 4)),
            dma,
            dma((4,)),
            dma((4,)),
            dma((4,)),
            dma((4,)),
            dma((3, 3)),
            dma((3, 3)),
            dma,
            dma,
            dma((3,)),
            dma((3,)),
            dma((3,)),
            dma((3,)),
            dma((2,)),
            dma((2,)),
            dma((2,)),
        ],
        compiler_params=pltpu.CompilerParams(
            collective_id=0, has_side_effects=True, vmem_limit_bytes=56 << 20
        ),
    )(tokens, seeds.reshape(16, 128), tile, gate_weight, up_weight)
    gate_new, gate_first_new, gate_second_new = adam_step(
        gate_weight, gate_first, gate_second, grad_gate
    )
    up_new, up_first_new, up_second_new = adam_step(up_weight, up_first, up_second, grad_up)
    return (hidden, gate_new, up_new, gate_first_new, up_first_new, gate_second_new, up_second_new)


def solution(mesh):
    spread = P("fsdp", "pop")
    return jax.shard_map(
        shards,
        mesh=mesh,
        in_specs=(P("pop", "fsdp"), P(), P(("pop", "fsdp"))) + (spread,) * 6,
        out_specs=(spread,) * 7,
        check_vma=False,
    )
```

profile of v0, /device:TPU:1, one launch (start us, length us, event | category | flops | bytes accessed | tf_op | source)
XLA Modules:
  0.0 138.9 jit_solution(13580284505809222476)
XLA Ops:
  0.6 0.0 copy-start.1
  0.6 0.0 copy-start
  0.7 0.8 tile.2
  1.5 0.1 broadcast_in_dim.7
  1.5 0.6 broadcast_in_dim.8.fitness
  2.1 1.7 %copy.16.tokens = bf16[256,320]{1,0:T(8,128)(2,1)} copy(bf16[256,320]{0,1:T(8,128)(2,1)} %param.9) | data formatting | bytes 327680 | tf_op args[0]
  3.9 124.5 %generation.1 = (bf16[128,1792]{1,0:T(8,128)(2,1)}, f32[320,1792]{1,0:T(8,128)}, f32[320,1792]{1,0:T(8,128)}) custom-call(bf16[256,320]{1,0:T(8,128)(2,1)} %copy.16.tokens, s32[16,128]{1,0:T(8,128)} %bitcast.1, f32[8,128]{1,0:T(8,128)} %broadcast_in_dim.8.fitness, bf16[320,1792]{1,0:T(8,128)(2,1)} %gate_w.1, bf16[320,1792]{1,0:T(8,128)(2,1)} %up_w.1), custom_call_target="tpu_custom_call" | custom-call | tf_op jit(solution)/shard_map/generation/pallas_call | solution.py:405
  128.4 0.0 copy-done.1
  128.4 0.0 copy-done
  128.4 0.0 copy-start.2
  128.4 9.7 %add_convert_fusion = (bf16[320,1792]{1,0:T(8,128)(2,1)}, f32[320,1792]{1,0:T(8,128)}, f32[320,1792]{1,0:T(8,128)}, bf16[320,1792]{1,0:T(8,128)(2,1)}, f32[320,1792]{1,0:T(8,128)}, /*index=5*/f32[320,1792]{1,0:T(8,128)}) fusion(bf16[320,1792]{1,0:T(8,128)(2,1)S(1)} %copy-done.1, f32[320,1792]{1,0:T(8,128)} %get-tuple-element.12, f32[320,1792]{1,0:T(8,128)} %param.15, ...), kind=kLoop, calls=%fused_computation.4 | loop fusion | flops 14909440 | bytes 27525120 | tf_op jit(solution)/shard_map/convert_element_type | solution.py:391
  138.1 0.0 copy-done.2
  138.1 0.8 copy.18
Async XLA Ops:
  0.6 127.7 %copy-start.1 = (bf16[320,1792]{1,0:T(8,128)(2,1)S(1)}, bf16[320,1792]{1,0:T(8,128)(2,1)}, u32[]{:S(2)}) copy-start(bf16[320,1792]{1,0:T(8,128)(2,1)} %up_w.1) | copy-start | bytes 3440644
  0.6 127.7 %copy-start = (bf16[320,1792]{1,0:T(8,128)(2,1)S(1)}, bf16[320,1792]{1,0:T(8,128)(2,1)}, u32[]{:S(2)}) copy-start(bf16[320,1792]{1,0:T(8,128)(2,1)} %gate_w.1) | copy-start | bytes 3440644
  128.4 9.7 %copy-start.2 = (bf16[128,1792]{1,0:T(8,128)(2,1)S(1)}, bf16[128,1792]{1,0:T(8,128)(2,1)}, u32[]{:S(2)}) copy-start(bf16[128,1792]{1,0:T(8,128)(2,1)} %get-tuple-element.29) | copy-start | bytes 1376260
where the time goes:
time: 139 us
  Pallas kernels  124 us (89%)
  other arithmetic  9.71 us (7%)
  local copies, waits for them, and re-layouts  4 us (3%)
    pallas_call x1, Pallas kernels, shards(): pl.pallas_call(kernel, name='generation', out_shape=(jax.ShapeDtypeStruct...  124 us
    convert_element_type x1, other arithmetic, adam_step(): return (moved.astype(jnp.bfloat16), first_new, second_new)  9.71 us

commit v1 on v0

--- a/solution.py
+++ b/solution.py
@@ -22,6 +22,7 @@
 SALT_STEP = 7919
 MIX = 73244475
 LEVELS = 32767.0
+EARLY = 3
 ROUNDER = 12582912.0
 
 
@@ -74,6 +75,10 @@
     sc,
     pr,
     sr,
+    fs,
+    fq,
+    fr,
+    fp,
     p0,
     lt,
     wt,
@@ -84,6 +89,8 @@
     r_xz,
     s_xx,
     r_xx,
+    s_xr,
+    r_xr,
     l_x,
     s_w,
     r_w,
@@ -97,6 +104,10 @@
     r_p,
     s_q,
     r_q,
+    s_f,
+    r_f,
+    s_g,
+    r_g,
     s_h,
     r_h,
     l_g,
@@ -105,10 +116,11 @@
     fsdp = lax.axis_index("fsdp")
     x, c = pop // 2, pop % 2
     y, z = fsdp // 4, fsdp % 4
-    width = tokens.shape[1]
-    half = wx.shape[3]
+    width = tokens.shape[0]
+    half = wx.shape[4]
     units = 2 * half
     z_core, z_half = z // 2, z % 2
+    split = width // 2
     partner = place(x, 1 - c, y, z)
 
     barrier = pltpu.get_barrier_semaphore()
@@ -128,27 +140,16 @@
 
     for d in (1, 3, 2):
         remote(tokens, xg.at[x, z], s_xz.at[d - 1], r_xz.at[d - 1], place(x, c, y, z + d)).start()
-    for d in (1, 3, 2):
+    for way in range(2):
         remote(
-            tokens, xg.at[x, z], s_xx.at[d - 1, 0], r_xx.at[d - 1, 0], place(x + d, c, y, z)
+            tokens,
+            xg.at[x, z],
+            s_xx.at[way, 0],
+            r_xx.at[way, 0],
+            place(x + 1 + 2 * way, c, y, z),
         ).start()
     own = pltpu.make_async_copy(tokens, xg.at[x, z], l_x)
     own.start()
-
-    def weight_send(cm, h):
-        src = (gate_w, up_w)[cm].at[:, pl.ds(h * half, half)]
-        mine = jnp.logical_and(c == cm, 2 * c + h == z)
-        away = remote(
-            src, wx.at[cm, z], s_w.at[2 * cm + h], r_w.at[z], place(x, cm, y, 2 * c + h)
-        )
-        here = pltpu.make_async_copy(src, wx.at[cm, z], r_w.at[z])
-        return mine, away, here
-
-    for h in range(2):
-        for cm in range(2):
-            mine, away, here = weight_send(cm, h)
-            pl.when(jnp.logical_not(mine))(away.start)
-            pl.when(mine)(here.start)
 
     eye = lax.broadcasted_iota(jnp.int32, (128, 128), 0) == lax.broadcasted_iota(
         jnp.int32, (128, 128), 1
@@ -156,17 +157,26 @@
     seed_mul[...] = seeds[...] * SEED_STEP
     my_info = info.at[c, y, x, z]
     my_info[...] = fitness[...]
-    left_columns = (
-        lax.broadcasted_iota(jnp.int32, (1, width), 1) + fsdp * width
-    ) * COLUMN_STEP
+    sub = lax.broadcasted_iota(jnp.int32, (32, 128), 0)
+    own.wait()
     for b in range(2):
-        seed_row = seeds[pl.ds(2 * pop + b, 1), :].astype(jnp.float32)
-        seed_col = column_of(seed_row, eye).astype(jnp.int32) * SEED_STEP
-        rows = tokens[b * 128 : (b + 1) * 128, :].astype(jnp.float32)
-        for k, salt in ((0, 1), (1, 3)):
-            left = levels_of(seed_col + (left_columns + salt * SALT_STEP))
-            along = jnp.sum(rows * left, axis=1, keepdims=True) * (1.0 / 128.0)
-            my_info[1 + 2 * k + b : 2 + 2 * k + b, :] = row_of(along, eye)
+        seed_row = seeds[pl.ds(2 * pop + b, 1), :] * SEED_STEP
+
+        def add_along(i, sums):
+            at = pl.ds(pl.multiple_of(i * 32, 32), 32)
+            rows = xg[x, z, at, b * 128 : (b + 1) * 128].astype(jnp.float32)
+            term = (sub + (fsdp * width + i * 32)) * COLUMN_STEP
+            return tuple(
+                kept + rows * levels_of(seed_row + (term + salt * SALT_STEP))
+                for kept, salt in zip(sums, (1, 3))
+            )
+
+        zero = jnp.zeros((32, 128), jnp.float32)
+        sums = lax.fori_loop(0, width // 32, add_along, (zero, zero))
+        for k in range(2):
+            my_info[1 + 2 * k + b : 2 + 2 * k + b, :] = jnp.sum(
+                sums[k], axis=0, keepdims=True
+            ) * (1.0 / 128.0)
 
     def info_send(stage, ref, d, device):
         return remote(ref, ref, s_i.at[stage, d - 1], r_i.at[stage, d - 1], device)
@@ -174,25 +184,56 @@
     for d in range(1, 4):
         info_send(0, info.at[c, y, x, z], d, place(x, c, y, z + d)).start()
 
+    def piece_of(source, j):
+        return xg.at[lax.rem(source, 4), lax.rem(z + 4 - j, 4)]
+
+    def over_x(piece, way, j):
+        there = place(x + 1 + 2 * way, c, y, z)
+        return remote(piece, piece, s_xx.at[way, j], r_xx.at[way, j], there)
+
+    def half_over_x(source, way, j):
+        piece = piece_of(source, j).at[way * split : (way + 1) * split]
+        there = place(x + 1 + 2 * way, c, y, z)
+        return remote(piece, piece, s_xr.at[way, j], r_xr.at[way, j], there)
+
     def forward(j):
-        piece = xg.at[x, lax.rem(z + 4 - j, 4)]
+        piece = piece_of(x, j)
         remote(piece, piece, s_xz.at[j - 1], r_xz.at[j - 1], place(x, c, y, z + j)).wait_recv()
-        for d in (1, 3, 2):
-            remote(
-                piece, piece, s_xx.at[d - 1, j], r_xx.at[d - 1, j], place(x + d, c, y, z)
-            ).start()
+        for way in range(2):
+            over_x(piece, way, j).start()
+
+    def relay(j):
+        for way in range(2):
+            source = x + 3 - 2 * way
+            over_x(piece_of(source, j), way, j).wait_recv()
+            half_over_x(source, way, j).start()
 
     def info_arrived(stage, ref_of):
         for d in range(1, 4):
             info_send(stage, ref_of(d), d, partner).wait_recv()
 
-    for j in (1, 3, 2):
-        forward(j)
+    def weight_send(k, h, r):
+        src = (gate_w, up_w)[k].at[r * split : (r + 1) * split, h * half : (h + 1) * half]
+        mine = jnp.logical_and(c == r, 2 * c + h == z)
+        away = remote(
+            src, wx.at[k, z, r], s_w.at[k, 2 * h + r], r_w.at[k, z], place(x, r, y, 2 * c + h)
+        )
+        here = pltpu.make_async_copy(src, wx.at[k, z, r], r_w.at[k, z])
+        return mine, away, here
+
+    for k in range(2):
+        for h in range(2):
+            for r in range(2):
+                mine, away, here = weight_send(k, h, r)
+                pl.when(jnp.logical_not(mine))(away.start)
+                pl.when(mine)(here.start)
+
     info_arrived(0, lambda d: info.at[c, y, x, lax.rem(z + 4 - d, 4)])
     for d in range(1, 4):
         info_send(1, info.at[c, y, x], d, place(x + d, c, y, z)).start()
-
-    sub = lax.broadcasted_iota(jnp.int32, (32, 128), 0)
+    for j in (1, 3, 2):
+        forward(j)
+    relay(0)
 
     def fill_left(k, salt):
         def body(i, _):
@@ -210,10 +251,14 @@
     info_arrived(1, lambda d: info.at[c, y, lax.rem(x + 4 - d, 4)])
     for d in range(1, 4):
         info_send(2, info.at[c, y], d, place(x, c, y + d, z)).start()
+    relay(1)
     fill_left(1, 3)
+    relay(3)
     info_arrived(2, lambda d: info.at[c, lax.rem(y + 4 - d, 4)])
     remote(info.at[c], info.at[c], s_ic, r_ic, partner).start()
     remote(info.at[1 - c], info.at[1 - c], s_ic, r_ic, partner).wait_recv()
+
+    relay(2)
 
     lane = lax.broadcasted_iota(jnp.int32, (1, 128), 1) // 16
     for r in range(16):
@@ -256,56 +301,95 @@
         lax.fori_loop(first, last, body, 0)
 
     chunks = units // chunk
-    gradient(0, 2, 0, chunks)
+
+    def weights_arrive(k):
+        for s in range(4):
+            mine = wx.at[k, s, c]
+            remote(mine, mine, s_w.at[k, 0], r_w.at[k, s], partner).wait_recv()
+            remote(mine, mine, s_c.at[k, s], r_c.at[k, s], partner).start()
+        for s in range(4):
+            other = wx.at[k, s, 1 - c]
+            remote(other, other, s_c.at[k, s], r_c.at[k, s], partner).wait_recv()
+
+    def rows_arrive():
+        for j in range(4):
+            for way in range(2):
+                half_over_x(x + 2, way, j).wait_recv()
+        for s in range(4):
+            xk[s] = xg[s].reshape(4 * width, 256).T
+
+    def product(k, d):
+        return jnp.dot(
+            xk[lax.rem(y + d, 4)],
+            wx[k].reshape(4 * width, half),
+            preferred_element_type=jnp.float32,
+        )
+
+    def code(k, b, codes, scales):
+        at = slice(b * 128, (b + 1) * 128)
+        top = jnp.max(jnp.abs(p0[0, k, at]), axis=1, keepdims=True)
+        top = jnp.maximum(top, 1e-30)
+        grown = p0[0, k, at] * (LEVELS / top)
+        whole_number = (grown + ROUNDER) - ROUNDER
+        codes[...] = whole_number.astype(jnp.int32).astype(jnp.int16)
+        scales[...] = row_of(top * (1.0 / LEVELS), eye)
+
+    def far_send(k, way):
+        there = place(x, c, y + 1 + 2 * way, z)
+        return (
+            remote(fs.at[k, way], fr.at[k, way], s_f.at[k, way], r_f.at[k, way], there),
+            remote(fq.at[k, way], fp.at[k, way], s_g.at[k, way], r_g.at[k, way], there),
+        )
+
+    def near_send(k, way):
+        there = place(x, c, y + 1 + 2 * way, z)
+        return (
+            remote(ps.at[k, way], pr.at[k, way], s_p.at[k, way], r_p.at[k, way], there),
+            remote(sc.at[k, way], sr.at[k, way], s_q.at[k, way], r_q.at[k, way], there),
+        )
+
+    def far(k):
+        p0[0, k] = product(k, 2)
+        for way in range(2):
+            code(k, way, fs.at[k, way], fq.at[k, way, 0:1])
+            for part in far_send(k, way):
+                part.start()
+
+    def near(k, way):
+        p0[0, k] = product(k, 1 + 2 * way)
+        for part in far_send(k, way):
+            part.wait_recv()
+        at = slice(way * 128, (way + 1) * 128)
+        step = column_of(fp[k, way, 0:1, :], eye)
+        p0[0, k, at] = p0[0, k, at] + fr[k, way].astype(jnp.int32).astype(jnp.float32) * step
+        for b in range(2):
+            code(k, b, ps.at[k, way, b * 128 : (b + 1) * 128], sc.at[k, way, b : b + 1])
+        for part in near_send(k, way):
+            part.start()
+
+    gradient(0, 2, 0, EARLY)
+    weights_arrive(0)
+    rows_arrive()
+    far(0)
+    weights_arrive(1)
+    far(1)
+    p0[1, 0] = product(0, 0)
+    p0[1, 1] = product(1, 0)
+    for k in range(2):
+        for way in range(2):
+            near(k, way)
+
+    gradient(0, 2, EARLY, chunks)
     copy_gate = pltpu.make_async_copy(gb.at[0], grad_gate, l_g.at[0])
     copy_gate.start()
-    gradient(1, 4, 0, 2)
-
-    for s in range(4):
-        remote(wx.at[c, s], wx.at[c, s], s_w.at[0], r_w.at[s], partner).wait_recv()
-        remote(wx.at[c, s], wx.at[c, s], s_c.at[s], r_c.at[s], partner).start()
-    own.wait()
-    for j in range(4):
-        for d in range(1, 4):
-            piece = xg.at[lax.rem(x + 4 - d, 4), lax.rem(z + 4 - j, 4)]
-            remote(
-                piece, piece, s_xx.at[d - 1, j], r_xx.at[d - 1, j], place(x + d, c, y, z)
-            ).wait_recv()
-    for s in range(4):
-        xk[s] = jnp.concatenate([xg[s, j] for j in range(4)], axis=1)
-    for s in range(4):
-        remote(wx.at[1 - c, s], wx.at[1 - c, s], s_c.at[s], r_c.at[s], partner).wait_recv()
-
-    for d in (2, 1, 3, 0):
-        to = lax.rem(y + d, 4)
-        rows = xk[to]
-        for k in range(2):
-            p0[:, k * half : (k + 1) * half] = jnp.dot(
-                rows, wx[k].reshape(4 * width, half), preferred_element_type=jnp.float32
-            )
-        if d == 0:
-            break
-        for b in range(2):
-            at = slice(b * 128, (b + 1) * 128)
-            for k in range(2):
-                over = slice(k * half, (k + 1) * half)
-                top = jnp.max(jnp.abs(p0[at, over]), axis=1, keepdims=True)
-                top = jnp.maximum(top, 1e-30)
-                grown = p0[at, over] * (LEVELS / top)
-                whole_number = (grown + ROUNDER) - ROUNDER
-                ps[d - 1, at, over] = whole_number.astype(jnp.int32).astype(jnp.int16)
-                sc[d - 1, 2 * k + b : 2 * k + b + 1, :] = row_of(top * (1.0 / LEVELS), eye)
-        there = place(x, c, y + d, z)
-        remote(ps.at[d - 1], pr.at[d - 1], s_p.at[d - 1], r_p.at[d - 1], there).start()
-        remote(sc.at[d - 1], sr.at[d - 1], s_q.at[d - 1], r_q.at[d - 1], there).start()
-
-    gradient(1, 4, 2, chunks)
+    gradient(1, 4, 0, chunks)
     copy_up = pltpu.make_async_copy(gb.at[1], grad_up, l_g.at[1])
     copy_up.start()
 
-    for d in (1, 3, 2):
-        remote(ps.at[d - 1], pr.at[d - 1], s_p.at[d - 1], r_p.at[d - 1], partner).wait_recv()
-        remote(sc.at[d - 1], sr.at[d - 1], s_q.at[d - 1], r_q.at[d - 1], partner).wait_recv()
+    for k in range(2):
+        for way in range(2):
+            for part in near_send(k, way):
+                part.wait_recv()
 
     first_unit = (2 * x + z_core) * units + z_half * half
     for b in range(2):
@@ -319,18 +403,15 @@
                 for zz in range(4):
                     row = row + info[c, yy, y, zz, 1 + 2 * k + b : 2 + 2 * k + b, :]
             along.append(column_of(row, eye) * noise_scale)
-        steps = [
-            [column_of(sr[d, 2 * k + b : 2 * k + b + 1, :], eye) for d in range(3)]
-            for k in range(2)
-        ]
+        steps = [[column_of(sr[k, d, b : b + 1, :], eye) for d in range(2)] for k in range(2)]
 
         def finish(j, _):
             out = []
             for k, salt in ((0, 2), (1, 4)):
-                over = pl.ds(pl.multiple_of(k * half + j * 128, 128), 128)
-                total = p0[at, over]
-                for d in range(3):
-                    total = total + pr[d, at, over].astype(jnp.int32).astype(
+                over = pl.ds(pl.multiple_of(j * 128, 128), 128)
+                total = p0[1, k, at, over]
+                for d in range(2):
+                    total = total + pr[k, d, at, over].astype(jnp.int32).astype(
                         jnp.float32
                     ) * steps[k][d]
                 columns = (
@@ -358,20 +439,25 @@
 
     for d in range(1, 4):
         remote(tokens, xg.at[x, z], s_xz.at[d - 1], r_xz.at[d - 1], partner).wait_send()
-        for j in range(4):
-            remote(tokens, xg.at[x, z], s_xx.at[d - 1, j], r_xx.at[d - 1, j], partner).wait_send()
         info_send(0, info.at[c, y, x, z], d, partner).wait_send()
         info_send(1, info.at[c, y, x], d, partner).wait_send()
         info_send(2, info.at[c, y], d, partner).wait_send()
-        remote(ps.at[d - 1], pr.at[d - 1], s_p.at[d - 1], r_p.at[d - 1], partner).wait_send()
-        remote(sc.at[d - 1], sr.at[d - 1], s_q.at[d - 1], r_q.at[d - 1], partner).wait_send()
+    for way in range(2):
+        for j in range(4):
+            over_x(piece_of(x, j), way, j).wait_send()
+            half_over_x(x + 2, way, j).wait_send()
+        for k in range(2):
+            for part in far_send(k, way) + near_send(k, way):
+                part.wait_send()
     remote(info.at[c], info.at[c], s_ic, r_ic, partner).wait_send()
-    for h in range(2):
-        for cm in range(2):
-            mine, away, here = weight_send(cm, h)
-            pl.when(jnp.logical_not(mine))(away.wait_send)
-    for s in range(4):
-        remote(wx.at[c, s], wx.at[c, s], s_c.at[s], r_c.at[s], partner).wait_send()
+    for k in range(2):
+        for h in range(2):
+            for r in range(2):
+                mine, away, here = weight_send(k, h, r)
+                pl.when(jnp.logical_not(mine))(away.wait_send)
+        for s in range(4):
+            mine = wx.at[k, s, c]
+            remote(mine, mine, s_c.at[k, s], r_c.at[k, s], partner).wait_send()
     for b in range(2):
         mine = jnp.logical_and(z_core == c, 2 * c + b == z)
         away = remote(
@@ -397,6 +483,7 @@
     width, units = gate_weight.shape
     half = units // 2
     rows = tokens.shape[0]
+    tokens = tokens.T
     bf, f32, i32, i16 = jnp.bfloat16, jnp.float32, jnp.int32, jnp.int16
     vmem = pl.BlockSpec(memory_space=pltpu.VMEM)
     anywhere = pl.BlockSpec(memory_space=pl.ANY)
@@ -410,20 +497,24 @@
             jax.ShapeDtypeStruct((width, units), f32),
             jax.ShapeDtypeStruct((width, units), f32),
         ),
-        in_specs=[vmem, vmem, vmem, anywhere, anywhere],
+        in_specs=[anywhere, vmem, vmem, anywhere, anywhere],
         out_specs=(vmem, anywhere, anywhere),
         scratch_shapes=[
-            pltpu.VMEM((4, 4, rows, width), bf),
+            pltpu.VMEM((4, 4, width, rows), bf),
             pltpu.VMEM((4, rows, 4 * width), bf),
-            pltpu.VMEM((2, 4, width, half), bf),
+            pltpu.VMEM((2, 4, 2, width // 2, half), bf),
             pltpu.VMEM((2, 4, 4, 4, 8, 128), f32),
             pltpu.VMEM((16, 128), i32),
             pltpu.VMEM((16, 128), f32),
-            pltpu.VMEM((3, rows, units), i16),
-            pltpu.VMEM((3, 8, 128), f32),
-            pltpu.VMEM((3, rows, units), i16),
-            pltpu.VMEM((3, 8, 128), f32),
-            pltpu.VMEM((rows, units), f32),
+            pltpu.VMEM((2, 2, rows, half), i16),
+            pltpu.VMEM((2, 2, 8, 128), f32),
+            pltpu.VMEM((2, 2, rows, half), i16),
+            pltpu.VMEM((2, 2, 8, 128), f32),
+            pltpu.VMEM((2, 2, rows // 2, half), i16),
+            pltpu.VMEM((2, 2, 8, 128), f32),
+            pltpu.VMEM((2, 2, rows // 2, half), i16),
+            pltpu.VMEM((2, 2, 8, 128), f32),
+            pltpu.VMEM((2, 2, rows, half), f32),
             pltpu.VMEM((2, width, MEMBERS), bf),
             pltpu.VMEM((256, MEMBERS), bf),
             pltpu.VMEM((2, width, units), f32),
@@ -431,21 +522,27 @@
             pltpu.VMEM((2, rows // 2, half), bf),
             dma((3,)),
             dma((3,)),
-            dma((3, 4)),
-            dma((3, 4)),
+            dma((2, 4)),
+            dma((2, 4)),
+            dma((2, 4)),
+            dma((2, 4)),
             dma,
-            dma((4,)),
-            dma((4,)),
-            dma((4,)),
-            dma((4,)),
+            dma((2, 4)),
+            dma((2, 4)),
+            dma((2, 4)),
+            dma((2, 4)),
             dma((3, 3)),
             dma((3, 3)),
             dma,
             dma,
-            dma((3,)),
-            dma((3,)),
-            dma((3,)),
-            dma((3,)),
+            dma((2, 2)),
+            dma((2, 2)),
+            dma((2, 2)),
+            dma((2, 2)),
+            dma((2, 2)),
+            dma((2, 2)),
+            dma((2, 2)),
+            dma((2, 2)),
             dma((2,)),
             dma((2,)),
             dma((2,)),

time: 139 us -> 97.3 us (0.70)
  Pallas kernels: 124 us -> 84.4 us
  local copies, waits for them, and re-layouts: 4 us -> 2.27 us
    pallas_call x1, Pallas kernels: 124 us -> 84.4 us  [shards(): pl.pallas_call(kernel, name='generation', out_shape=(jax.ShapeDtypeStruct...]
    unnamed x8 -> x7, local copies, waits for them, and re-layouts: 2.52 us -> 0.79 us
where the time goes in v1:
time: 97.3 us; the launch traced here: 97.1 us
  Pallas kernels  84.4 us (87%)
  other arithmetic  9.71 us (10%)
  local copies, waits for them, and re-layouts  2.27 us (2%)
    pallas_call x1, Pallas kernels, shards(): pl.pallas_call(kernel, name='generation', out_shape=(jax.ShapeDtypeStruct...  84.4 us
    convert_element_type x1, other arithmetic, adam_step(): return (moved.astype(jnp.bfloat16), first_new, second_new)  9.71 us

profile of v1, /device:TPU:1, one launch (start us, length us, event | category | flops | bytes accessed | tf_op | source)
XLA Modules:
  0.0 97.1 jit_solution(11906236214019098279)
XLA Ops:
  0.6 0.0 copy-start.1
  0.6 0.0 copy-start
  0.7 0.8 tile.2
  1.5 0.1 broadcast_in_dim.7
  1.5 0.6 broadcast_in_dim.8.fitness
  2.1 84.4 %generation.1 = (bf16[128,1792]{1,0:T(8,128)(2,1)}, f32[320,1792]{1,0:T(8,128)}, f32[320,1792]{1,0:T(8,128)}) custom-call(bf16[320,256]{1,0:T(8,128)(2,1)} %bitcast.2, s32[16,128]{1,0:T(8,128)} %bitcast.3, f32[8,128]{1,0:T(8,128)} %broadcast_in_dim.8.fitness, bf16[320,1792]{1,0:T(8,128)(2,1)} %gate_w.1, bf16[320,1792]{1,0:T(8,128)(2,1)} %up_w.1), custom_call_target="tpu_custom_call" | custom-call | tf_op jit(solution)/shard_map/generation/pallas_call | solution.py:492
  86.6 0.0 copy-done.1
  86.6 0.0 copy-done
  86.6 0.0 copy-start.2
  86.6 9.7 %add_convert_fusion = (bf16[320,1792]{1,0:T(8,128)(2,1)}, f32[320,1792]{1,0:T(8,128)}, f32[320,1792]{1,0:T(8,128)}, bf16[320,1792]{1,0:T(8,128)(2,1)}, f32[320,1792]{1,0:T(8,128)}, /*index=5*/f32[320,1792]{1,0:T(8,128)}) fusion(bf16[320,1792]{1,0:T(8,128)(2,1)S(1)} %copy-done.1, f32[320,1792]{1,0:T(8,128)} %get-tuple-element.12, f32[320,1792]{1,0:T(8,128)} %param.15, ...), kind=kLoop, calls=%fused_computation.4 | loop fusion | flops 14909440 | bytes 27525120 | tf_op jit(solution)/shard_map/convert_element_type | solution.py:477
  96.3 0.0 copy-done.2
  96.3 0.8 copy.17
Async XLA Ops:
  0.6 86.0 %copy-start.1 = (bf16[320,1792]{1,0:T(8,128)(2,1)S(1)}, bf16[320,1792]{1,0:T(8,128)(2,1)}, u32[]{:S(2)}) copy-start(bf16[320,1792]{1,0:T(8,128)(2,1)} %up_w.1) | copy-start | bytes 3440644
  0.6 86.0 %copy-start = (bf16[320,1792]{1,0:T(8,128)(2,1)S(1)}, bf16[320,1792]{1,0:T(8,128)(2,1)}, u32[]{:S(2)}) copy-start(bf16[320,1792]{1,0:T(8,128)(2,1)} %gate_w.1) | copy-start | bytes 3440644
  86.6 9.7 %copy-start.2 = (bf16[128,1792]{1,0:T(8,128)(2,1)S(1)}, bf16[128,1792]{1,0:T(8,128)(2,1)}, u32[]{:S(2)}) copy-start(bf16[128,1792]{1,0:T(8,128)(2,1)} %get-tuple-element.29) | copy-start | bytes 1376260

commit v2 on v1

--- a/solution.py
+++ b/solution.py
@@ -156,7 +156,9 @@
     )
     seed_mul[...] = seeds[...] * SEED_STEP
     my_info = info.at[c, y, x, z]
-    my_info[...] = fitness[...]
+    my_info[...] = jnp.zeros((8, 128), jnp.float32)
+    my_info[0:1, 0:16] = fitness[...]
+    my_info[...] = pltpu.roll(my_info[...], 16 * lax.rem(fsdp, 8), 1)
     sub = lax.broadcasted_iota(jnp.int32, (32, 128), 0)
     own.wait()
     for b in range(2):
@@ -228,12 +230,13 @@
                 pl.when(jnp.logical_not(mine))(away.start)
                 pl.when(mine)(here.start)
 
+    forward(1)
+    forward(3)
+    relay(0)
     info_arrived(0, lambda d: info.at[c, y, x, lax.rem(z + 4 - d, 4)])
     for d in range(1, 4):
         info_send(1, info.at[c, y, x], d, place(x + d, c, y, z)).start()
-    for j in (1, 3, 2):
-        forward(j)
-    relay(0)
+    forward(2)
 
     def fill_left(k, salt):
         def body(i, _):
@@ -248,17 +251,16 @@
         lax.fori_loop(0, width // 32, body, 0)
 
     fill_left(0, 1)
+    relay(1)
+    relay(3)
     info_arrived(1, lambda d: info.at[c, y, lax.rem(x + 4 - d, 4)])
     for d in range(1, 4):
         info_send(2, info.at[c, y], d, place(x, c, y + d, z)).start()
-    relay(1)
     fill_left(1, 3)
-    relay(3)
     info_arrived(2, lambda d: info.at[c, lax.rem(y + 4 - d, 4)])
     remote(info.at[c], info.at[c], s_ic, r_ic, partner).start()
+    relay(2)
     remote(info.at[1 - c], info.at[1 - c], s_ic, r_ic, partner).wait_recv()
-
-    relay(2)
 
     lane = lax.broadcasted_iota(jnp.int32, (1, 128), 1) // 16
     for r in range(16):
@@ -302,11 +304,13 @@
 
     chunks = units // chunk
 
-    def weights_arrive(k):
+    def weights_share(k):
         for s in range(4):
             mine = wx.at[k, s, c]
             remote(mine, mine, s_w.at[k, 0], r_w.at[k, s], partner).wait_recv()
             remote(mine, mine, s_c.at[k, s], r_c.at[k, s], partner).start()
+
+    def weights_arrive(k):
         for s in range(4):
             other = wx.at[k, s, 1 - c]
             remote(other, other, s_c.at[k, s], r_c.at[k, s], partner).wait_recv()
@@ -315,12 +319,13 @@
         for j in range(4):
             for way in range(2):
                 half_over_x(x + 2, way, j).wait_recv()
-        for s in range(4):
-            xk[s] = xg[s].reshape(4 * width, 256).T
+
+    def turn(d):
+        xk[d] = xg[lax.rem(y + d, 4)].reshape(4 * width, 256).T
 
     def product(k, d):
         return jnp.dot(
-            xk[lax.rem(y + d, 4)],
+            xk[d],
             wx[k].reshape(4 * width, half),
             preferred_element_type=jnp.float32,
         )
@@ -341,11 +346,15 @@
             remote(fq.at[k, way], fp.at[k, way], s_g.at[k, way], r_g.at[k, way], there),
         )
 
-    def near_send(k, way):
+    def near_send(k, way, b):
         there = place(x, c, y + 1 + 2 * way, z)
         return (
-            remote(ps.at[k, way], pr.at[k, way], s_p.at[k, way], r_p.at[k, way], there),
-            remote(sc.at[k, way], sr.at[k, way], s_q.at[k, way], r_q.at[k, way], there),
+            remote(
+                ps.at[k, way, b], pr.at[k, way, b], s_p.at[k, way, b], r_p.at[k, way, b], there
+            ),
+            remote(
+                sc.at[k, way, b], sr.at[k, way, b], s_q.at[k, way, b], r_q.at[k, way, b], there
+            ),
         )
 
     def far(k):
@@ -363,21 +372,28 @@
         step = column_of(fp[k, way, 0:1, :], eye)
         p0[0, k, at] = p0[0, k, at] + fr[k, way].astype(jnp.int32).astype(jnp.float32) * step
         for b in range(2):
-            code(k, b, ps.at[k, way, b * 128 : (b + 1) * 128], sc.at[k, way, b : b + 1])
-        for part in near_send(k, way):
-            part.start()
+            code(k, b, ps.at[k, way, b], sc.at[k, way, b, 0:1])
+            for part in near_send(k, way, b):
+                part.start()
 
     gradient(0, 2, 0, EARLY)
+    weights_share(0)
+    rows_arrive()
+    turn(2)
     weights_arrive(0)
-    rows_arrive()
     far(0)
+    weights_share(1)
+    turn(0)
+    p0[1, 0] = product(0, 0)
     weights_arrive(1)
     far(1)
-    p0[1, 0] = product(0, 0)
+    turn(1)
+    near(0, 0)
+    turn(3)
+    near(0, 1)
     p0[1, 1] = product(1, 0)
-    for k in range(2):
-        for way in range(2):
-            near(k, way)
+    near(1, 0)
+    near(1, 1)
 
     gradient(0, 2, EARLY, chunks)
     copy_gate = pltpu.make_async_copy(gb.at[0], grad_gate, l_g.at[0])
@@ -386,13 +402,12 @@
     copy_up = pltpu.make_async_copy(gb.at[1], grad_up, l_g.at[1])
     copy_up.start()
 
-    for k in range(2):
-        for way in range(2):
-            for part in near_send(k, way):
-                part.wait_recv()
-
     first_unit = (2 * x + z_core) * units + z_half * half
     for b in range(2):
+        for k in range(2):
+            for way in range(2):
+                for part in near_send(k, way, b):
+                    part.wait_recv()
         at = slice(b * 128, (b + 1) * 128)
         seed_row = seeds[pl.ds(2 * (2 * y + c) + b, 1), :].astype(jnp.float32)
         seed_col = column_of(seed_row, eye).astype(jnp.int32) * SEED_STEP
@@ -403,7 +418,7 @@
                 for zz in range(4):
                     row = row + info[c, yy, y, zz, 1 + 2 * k + b : 2 + 2 * k + b, :]
             along.append(column_of(row, eye) * noise_scale)
-        steps = [[column_of(sr[k, d, b : b + 1, :], eye) for d in range(2)] for k in range(2)]
+        steps = [[column_of(sr[k, d, b, 0:1, :], eye) for d in range(2)] for k in range(2)]
 
         def finish(j, _):
             out = []
@@ -411,7 +426,7 @@
                 over = pl.ds(pl.multiple_of(j * 128, 128), 128)
                 total = p0[1, k, at, over]
                 for d in range(2):
-                    total = total + pr[k, d, at, over].astype(jnp.int32).astype(
+                    total = total + pr[k, d, b, :, over].astype(jnp.int32).astype(
                         jnp.float32
                     ) * steps[k][d]
                 columns = (
@@ -447,7 +462,7 @@
             over_x(piece_of(x, j), way, j).wait_send()
             half_over_x(x + 2, way, j).wait_send()
         for k in range(2):
-            for part in far_send(k, way) + near_send(k, way):
+            for part in far_send(k, way) + near_send(k, way, 0) + near_send(k, way, 1):
                 part.wait_send()
     remote(info.at[c], info.at[c], s_ic, r_ic, partner).wait_send()
     for k in range(2):
@@ -488,7 +503,6 @@
     vmem = pl.BlockSpec(memory_space=pltpu.VMEM)
     anywhere = pl.BlockSpec(memory_space=pl.ANY)
     dma = pltpu.SemaphoreType.DMA
-    tile = jnp.broadcast_to(jnp.tile(fitness, 8)[None], (8, 128))
     hidden, grad_gate, grad_up = pl.pallas_call(
         kernel,
         name="generation",
@@ -506,10 +520,10 @@
             pltpu.VMEM((2, 4, 4, 4, 8, 128), f32),
             pltpu.VMEM((16, 128), i32),
             pltpu.VMEM((16, 128), f32),
-            pltpu.VMEM((2, 2, rows, half), i16),
-            pltpu.VMEM((2, 2, 8, 128), f32),
-            pltpu.VMEM((2, 2, rows, half), i16),
-            pltpu.VMEM((2, 2, 8, 128), f32),
+            pltpu.VMEM((2, 2, 2, rows // 2, half), i16),
+            pltpu.VMEM((2, 2, 2, 8, 128), f32),
+            pltpu.VMEM((2, 2, 2, rows // 2, half), i16),
+            pltpu.VMEM((2, 2, 2, 8, 128), f32),
             pltpu.VMEM((2, 2, rows // 2, half), i16),
             pltpu.VMEM((2, 2, 8, 128), f32),
             pltpu.VMEM((2, 2, rows // 2, half), i16),
@@ -535,10 +549,10 @@
             dma((3, 3)),
             dma,
             dma,
-            dma((2, 2)),
-            dma((2, 2)),
-            dma((2, 2)),
-            dma((2, 2)),
+            dma((2, 2, 2)),
+            dma((2, 2, 2)),
+            dma((2, 2, 2)),
+            dma((2, 2, 2)),
             dma((2, 2)),
             dma((2, 2)),
             dma((2, 2)),
@@ -550,7 +564,7 @@
         compiler_params=pltpu.CompilerParams(
             collective_id=0, has_side_effects=True, vmem_limit_bytes=56 << 20
         ),
-    )(tokens, seeds.reshape(16, 128), tile, gate_weight, up_weight)
+    )(tokens, seeds.reshape(16, 128), fitness.reshape(1, 16), gate_weight, up_weight)
     gate_new, gate_first_new, gate_second_new = adam_step(
         gate_weight, gate_first, gate_second, grad_gate
     )

time: 97.3 us -> 93.1 us (0.957)
  Pallas kernels: 84.4 us -> 81.7 us
  local copies, waits for them, and re-layouts: 2.27 us -> 0.78 us
    pallas_call x1, Pallas kernels: 84.4 us -> 81.7 us  [shards(): pl.pallas_call(kernel, name='generation', out_shape=(jax.ShapeDtypeStruct...]
where the time goes in v2:
time: 93.1 us; the launch traced here: 92.9 us
  Pallas kernels  81.7 us (88%)
  other arithmetic  9.71 us (10%)
    pallas_call x1, Pallas kernels, shards(): pl.pallas_call(kernel, name='generation', out_shape=(jax.ShapeDtypeStruct...  81.7 us
    convert_element_type x1, other arithmetic, adam_step(): return (moved.astype(jnp.bfloat16), first_new, second_new)  9.71 us

profile of v2, /device:TPU:1, one launch (start us, length us, event | category | flops | bytes accessed | tf_op | source)
XLA Modules:
  0.0 92.9 jit_solution(7690549558365573937)
XLA Ops:
  0.6 0.0 copy-start.1
  0.6 0.0 copy-start
  0.7 81.7 %generation.1 = (bf16[128,1792]{1,0:T(8,128)(2,1)}, f32[320,1792]{1,0:T(8,128)}, f32[320,1792]{1,0:T(8,128)}) custom-call(bf16[320,256]{1,0:T(8,128)(2,1)} %bitcast.3, s32[16,128]{1,0:T(8,128)} %bitcast.4, f32[1,16]{1,0:T(1,128)} %bitcast.5, bf16[320,1792]{1,0:T(8,128)(2,1)} %gate_w.1, bf16[320,1792]{1,0:T(8,128)(2,1)} %up_w.1), custom_call_target="tpu_custom_call" | custom-call | tf_op jit(solution)/shard_map/generation/pallas_call | solution.py:506
  82.3 0.0 copy-done.1
  82.3 0.0 copy-done
  82.4 0.0 copy-start.2
  82.4 9.7 %add_convert_fusion = (bf16[320,1792]{1,0:T(8,128)(2,1)}, f32[320,1792]{1,0:T(8,128)}, f32[320,1792]{1,0:T(8,128)}, bf16[320,1792]{1,0:T(8,128)(2,1)}, f32[320,1792]{1,0:T(8,128)}, /*index=5*/f32[320,1792]{1,0:T(8,128)}) fusion(bf16[320,1792]{1,0:T(8,128)(2,1)S(1)} %copy-done.1, f32[320,1792]{1,0:T(8,128)} %get-tuple-element.12, f32[320,1792]{1,0:T(8,128)} %param.15, ...), kind=kLoop, calls=%fused_computation.4 | loop fusion | flops 14909440 | bytes 27525120 | tf_op jit(solution)/shard_map/convert_element_type | solution.py:492
  92.1 0.0 copy-done.2
  92.1 0.8 copy.17
Async XLA Ops:
  0.6 81.7 %copy-start.1 = (bf16[320,1792]{1,0:T(8,128)(2,1)S(1)}, bf16[320,1792]{1,0:T(8,128)(2,1)}, u32[]{:S(2)}) copy-start(bf16[320,1792]{1,0:T(8,128)(2,1)} %up_w.1) | copy-start | bytes 3440644
  0.6 81.7 %copy-start = (bf16[320,1792]{1,0:T(8,128)(2,1)S(1)}, bf16[320,1792]{1,0:T(8,128)(2,1)}, u32[]{:S(2)}) copy-start(bf16[320,1792]{1,0:T(8,128)(2,1)} %gate_w.1) | copy-start | bytes 3440644
  82.4 9.7 %copy-start.2 = (bf16[128,1792]{1,0:T(8,128)(2,1)S(1)}, bf16[128,1792]{1,0:T(8,128)(2,1)}, u32[]{:S(2)}) copy-start(bf16[128,1792]{1,0:T(8,128)(2,1)} %get-tuple-element.29) | copy-start | bytes 1376260

commit v3 on v2

--- a/solution.py
+++ b/solution.py
@@ -291,7 +291,7 @@
                     ).astype(jnp.bfloat16)
                 return 0
 
-            lax.fori_loop(0, chunk // 32, fill, 0)
+            lax.fori_loop(0, chunk // 32, fill, 0, unroll=2)
             total = lax.dot_general(
                 lt[k], wt[...], (((1,), (1,)), ((), ())), preferred_element_type=jnp.float32
             )

time: 93.1 us -> 93.1 us (level)
  no operation moved by 1% of the time
where the time goes in v3:
time: 93.1 us; the launch traced here: 92.8 us
  Pallas kernels  81.6 us (88%)
  other arithmetic  9.71 us (10%)
    pallas_call x1, Pallas kernels, shards(): pl.pallas_call(kernel, name='generation', out_shape=(jax.ShapeDtypeStruct...  81.6 us
    convert_element_type x1, other arithmetic, adam_step(): return (moved.astype(jnp.bfloat16), first_new, second_new)  9.71 us

profile of v3, /device:TPU:1, one launch (start us, length us, event | category | flops | bytes accessed | tf_op | source)
XLA Modules:
  0.0 92.8 jit_solution(13801978196216400378)
XLA Ops:
  0.6 0.0 copy-start.1
  0.6 0.0 copy-start
  0.7 81.6 %generation.1 = (bf16[128,1792]{1,0:T(8,128)(2,1)}, f32[320,1792]{1,0:T(8,128)}, f32[320,1792]{1,0:T(8,128)}) custom-call(bf16[320,256]{1,0:T(8,128)(2,1)} %bitcast.3, s32[16,128]{1,0:T(8,128)} %bitcast.4, f32[1,16]{1,0:T(1,128)} %bitcast.5, bf16[320,1792]{1,0:T(8,128)(2,1)} %gate_w.1, bf16[320,1792]{1,0:T(8,128)(2,1)} %up_w.1), custom_call_target="tpu_custom_call" | custom-call | tf_op jit(solution)/shard_map/generation/pallas_call | solution.py:506
  82.3 0.0 copy-done.1
  82.3 0.0 copy-done
  82.3 0.0 copy-start.2
  82.3 9.7 %add_convert_fusion = (bf16[320,1792]{1,0:T(8,128)(2,1)}, f32[320,1792]{1,0:T(8,128)}, f32[320,1792]{1,0:T(8,128)}, bf16[320,1792]{1,0:T(8,128)(2,1)}, f32[320,1792]{1,0:T(8,128)}, /*index=5*/f32[320,1792]{1,0:T(8,128)}) fusion(bf16[320,1792]{1,0:T(8,128)(2,1)S(1)} %copy-done.1, f32[320,1792]{1,0:T(8,128)} %get-tuple-element.12, f32[320,1792]{1,0:T(8,128)} %param.15, ...), kind=kLoop, calls=%fused_computation.4 | loop fusion | flops 14909440 | bytes 27525120 | tf_op jit(solution)/shard_map/convert_element_type | solution.py:492
  92.0 0.0 copy-done.2
  92.0 0.8 copy.17
Async XLA Ops:
  0.6 81.6 %copy-start.1 = (bf16[320,1792]{1,0:T(8,128)(2,1)S(1)}, bf16[320,1792]{1,0:T(8,128)(2,1)}, u32[]{:S(2)}) copy-start(bf16[320,1792]{1,0:T(8,128)(2,1)} %up_w.1) | copy-start | bytes 3440644
  0.6 81.6 %copy-start = (bf16[320,1792]{1,0:T(8,128)(2,1)S(1)}, bf16[320,1792]{1,0:T(8,128)(2,1)}, u32[]{:S(2)}) copy-start(bf16[320,1792]{1,0:T(8,128)(2,1)} %gate_w.1) | copy-start | bytes 3440644
  82.3 9.7 %copy-start.2 = (bf16[128,1792]{1,0:T(8,128)(2,1)S(1)}, bf16[128,1792]{1,0:T(8,128)(2,1)}, u32[]{:S(2)}) copy-start(bf16[128,1792]{1,0:T(8,128)(2,1)} %get-tuple-element.29) | copy-start | bytes 1376260
